TPU v7x, 32 devices: a whole 2x2x4 slice. The times are simulated.
32 devices in a mesh: section: 4 (over x, core), col: 4 (over z), row: 2 (over y).
Axes of the slice: x: 2, y: 2, z: 4, core: 2. Of those that a mesh axis runs over, the one named last changes fastest.
Arguments:
- features: bfloat16 [4, 32, 128, 256], P(None, 'row', 'col'), may hold values from -6 to 6
- conv_weight: bfloat16 [4, 3, 3, 256, 256], P('section'), may hold values from -0.125 to 0.125
- tissue: int32 [4, 32, 128], P(None, 'row', 'col'), may hold values 0 or 1
Outputs:
- section_out: bfloat16 [4, 4, 32, 128, 256], P('section', None, 'row', 'col')
- loss_map: float32 [4, 4, 32, 128], P('section', None, 'row', 'col')
All inputs are finite; a program needn't handle non-finite values. No bound on the sum of `tissue` on one device may be relied on, other than what follows from the above.
Results may differ from a plain program's by a relative error of at most 0.008.
Values may be sent and summed in bfloat16 or wider, within the bound.
A program may use at most 64 MiB of HBM per device.

v0:
```python
import jax
import jax.numpy as jnp
from jax import lax
from jax.sharding import PartitionSpec as P

DILATION_RATE = 2


residual_scale = 0.8


def with_halo(value, sides, width):
    for axis, dim in sides:
        devices, length = (lax.axis_size(axis), value.shape[dim])
        up = [(i, (i + 1) % devices) for i in range(devices - 1)]
        down = [(j, i) for i, j in up]
        last = lax.slice_in_dim(value, length - width, length, axis=dim)
        first = lax.slice_in_dim(value, 0, width, axis=dim)
        before = lax.ppermute(last, axis, up)
        after = lax.ppermute(first, axis, down)
        value = jnp.concatenate([before, value, after], axis=dim)
    return value


def from_behind(value, axis, by):
    devices = lax.axis_size(axis)
    pairs = [(i, i + by) for i in range(devices) if 0 <= i + by < devices]
    return lax.ppermute(value, axis, pairs)


def local(features, conv_weight, tissue):
    section_count = lax.axis_size("section")
    section_index = lax.axis_index("section")
    micro_count, row_cell_total, column_cell_total, channels = features.shape
    cell_count = row_cell_total * column_cell_total
    filter_weight = conv_weight[0]
    alt_kernel = filter_weight[:, ::-1]

    def apply_layer(paired_batch):
        padded_activation = with_halo(paired_batch, (("col", 2), ("row", 1)), DILATION_RATE)
        acc_main = jnp.zeros((cell_count, channels), jnp.float32)
        acc_flip = jnp.zeros((cell_count, channels), jnp.float32)
        for vertical_offset in range(3):
            for horizontal_offset in range(3):
                shifted = padded_activation[
                    :,
                    DILATION_RATE * vertical_offset : DILATION_RATE * vertical_offset
                    + row_cell_total,
                    DILATION_RATE * horizontal_offset : DILATION_RATE * horizontal_offset
                    + column_cell_total,
                    :,
                ]
                acc_main = acc_main + jnp.dot(
                    shifted[0].reshape(cell_count, channels),
                    filter_weight[vertical_offset, horizontal_offset],
                    preferred_element_type=jnp.float32,
                )
                acc_flip = acc_flip + jnp.dot(
                    shifted[1].reshape(cell_count, channels),
                    alt_kernel[vertical_offset, horizontal_offset],
                    preferred_element_type=jnp.float32,
                )
        hidden_features = jnp.stack([acc_main, acc_flip]).reshape(
            2, row_cell_total, column_cell_total, channels
        )
        return (
            residual_scale * (paired_batch.astype(jnp.float32) + jnp.maximum(hidden_features, 0.0))
        ).astype(jnp.bfloat16)

    def advance(time_step, carried):
        incoming, stored, losses = carried
        entry_index = jnp.clip(time_step, 0, micro_count - 1)
        entering = jnp.stack(
            [
                lax.dynamic_index_in_dim(features, entry_index, 0, keepdims=False),
                lax.dynamic_index_in_dim(features, entry_index, 0, keepdims=False),
            ]
        )
        paired_batch = jnp.where(section_index == 0, entering, incoming)
        result = apply_layer(paired_batch)
        restored = result[1]
        slot_index = time_step - section_index
        is_valid = jnp.logical_and(slot_index >= 0, slot_index < micro_count)
        write_index = jnp.clip(slot_index, 0, micro_count - 1)
        mask_float = lax.dynamic_index_in_dim(tissue, write_index, 0, keepdims=False).astype(
            jnp.float32
        )
        deviation = result[0].astype(jnp.float32) - restored.astype(jnp.float32)
        loss_term = mask_float * jnp.mean(deviation * deviation, -1)
        old_out = lax.dynamic_index_in_dim(stored, write_index, 0, keepdims=False)
        old_loss = lax.dynamic_index_in_dim(losses, write_index, 0, keepdims=False)
        stored = lax.dynamic_update_index_in_dim(
            stored, jnp.where(is_valid, result[0], old_out), write_index, 0
        )
        losses = lax.dynamic_update_index_in_dim(
            losses, jnp.where(is_valid, loss_term, old_loss), write_index, 0
        )
        outgoing = from_behind(result, "section", 1)
        return (outgoing, stored, losses)

    initial = (
        jnp.zeros((2, row_cell_total, column_cell_total, channels), jnp.bfloat16),
        jnp.zeros((micro_count, row_cell_total, column_cell_total, channels), jnp.bfloat16),
        jnp.zeros((micro_count, row_cell_total, column_cell_total), jnp.float32),
    )
    final_state = lax.fori_loop(0, micro_count + section_count - 1, advance, initial)
    return (final_state[1][None], final_state[2][None])


def solution(mesh):
    return jax.shard_map(
        local,
        mesh=mesh,
        in_specs=(
            P(None, "row", "col", None),
            P("section", None, None, None, None),
            P(None, "row", "col"),
        ),
        out_specs=(P("section", None, "row", "col", None), P("section", None, "row", "col")),
        check_vma=False,
    )
```

profile of v0, /device:TPU:26, one launch (start us, length us, event | category | flops | bytes accessed | tf_op | source)
XLA Modules:
  0.0 236.0 jit_solution(1295545915450604533)
XLA Ops:
  0.6 2.4 %rev.3 = bf16[3,3,256,256]{3,2,1,0:T(8,128)(2,1)} reverse(bf16[3,3,256,256]{3,2,1,0:T(8,128)(2,1)} %bitcast.217), dimensions={1} | reverse | bytes 2359296 | tf_op jit(solution)/shard_map/rev | solution.py:37
  4.6 230.8 %while.18 = (s32[]{:T(128)}, bf16[2,16,32,256]{3,2,1,0:T(8,128)(2,1)S(1)}, bf16[4,16,32,256]{3,2,1,0:T(8,128)(2,1)}, f32[4,16,32]{2,1,0:T(8,128)S(1)}, pred[]{:T...) while((s32[]{:T(128)}, ...), condition=%wide.region_2.3_spmd, body=%wide.region_0.2_spmd.sunk | while | flops 1221314048 | bytes 50016708 | solution.py:106
  5.8 2.4 collective-permute-start
  8.1 1.3 collective-permute-start.1
  9.7 4.2 %collective-permute-done.1 = bf16[2,16,2,256]{3,2,1,0:T(2,128)(2,1)S(1)} collective-permute-done((bf16[2,16,2,256]{3,2,1,0:T(2,128)(2,1)S(1)}, bf16[2,16,2,256]{3,2,1,0:T(2,128)(2,1)S(1)}, u32[]{:S(2)}, u32[]{:S(2)}) %collective-permute-start.1) | collective-permute-done | bytes 32800 | tf_op jit(solution)/shard_map/while/body/eval_jaxpr/ppermute | solution.py:19
  14.0 3.4 %collective-permute-start.2 = (bf16[2,2,36,256]{3,2,1,0:T(8,128)(2,1)S(1)}, bf16[2,2,36,256]{3,2,1,0:T(8,128)(2,1)S(1)}, u32[]{:S(2)}, u32[]{:S(2)}) collective-permute-start(bf16[2,2,36,256]{3,2,1,0:T(8,128)(2,1)S(1)} %get-tuple-element.339), channel_id=1, source_target_pairs={{0,1},{2,3},{4,5},{6,7},{8,9},{10,11},{12,13},{14,15},{16,17},{18,... | collective-permute-start | bytes 221192 | tf_op jit(solution)/shard_map/while/body/eval_jaxpr/ppermute | solution.py:19
  17.4 1.4 collective-permute-start.3
  19.9 4.0 %collective-permute-done.3 = bf16[2,2,36,256]{3,2,1,0:T(8,128)(2,1)S(1)} collective-permute-done((bf16[2,2,36,256]{3,2,1,0:T(8,128)(2,1)S(1)}, bf16[2,2,36,256]{3,2,1,0:T(8,128)(2,1)S(1)}, u32[]{:S(2)}, u32[]{:S(2)}) %collective-permute-start.3) | collective-permute-done | bytes 73760 | tf_op jit(solution)/shard_map/while/body/eval_jaxpr/ppermute | solution.py:20
  28.9 1.9 collective-permute-start.4
  31.7 1.7 select_dynamic-update-slice_fusion.2
  33.5 6.0 %collective-permute-done.4 = bf16[2,16,32,256]{3,2,1,0:T(8,128)(2,1)S(1)} collective-permute-done((bf16[2,16,32,256]{3,2,1,0:T(8,128)(2,1)S(1)}, bf16[2,16,32,256]{3,2,1,0:T(8,128)(2,1)S(1)}, u32[]{:S(2)}, u32[]{:S(2)}) %collective-permute-start.4) | collective-permute-done | bytes 524320 | tf_op jit(solution)/shard_map/while/body/eval_jaxpr/ppermute | solution.py:28
  40.5 2.4 %collective-permute-start = (bf16[2,16,2,256]{3,2,1,0:T(2,128)(2,1)S(1)}, bf16[2,16,2,256]{3,2,1,0:T(2,128)(2,1)S(1)}, u32[]{:S(2)}, u32[]{:S(2)}) collective-permute-start(bf16[2,16,2,256]{3,2,1,0:T(2,128)(2,1)S(1)} %get-tuple-element.337), channel_id=1, source_target_pairs={{2,0},{4,2},{6,4},{3,1},{5,3},{7,5},{10,8},{12,10},{14,12},{11,9},... | collective-permute-start | bytes 98312 | tf_op jit(solution)/shard_map/while/body/eval_jaxpr/ppermute | solution.py:20
  43.0 1.3 collective-permute-start.1
  44.5 4.2 %collective-permute-done.1 = bf16[2,16,2,256]{3,2,1,0:T(2,128)(2,1)S(1)} collective-permute-done((bf16[2,16,2,256]{3,2,1,0:T(2,128)(2,1)S(1)}, bf16[2,16,2,256]{3,2,1,0:T(2,128)(2,1)S(1)}, u32[]{:S(2)}, u32[]{:S(2)}) %collective-permute-start.1) | collective-permute-done | bytes 32800 | tf_op jit(solution)/shard_map/while/body/eval_jaxpr/ppermute | solution.py:19
  48.8 1.5 collective-permute-start.2
  50.4 1.4 collective-permute-start.3
  52.8 4.0 %collective-permute-done.3 = bf16[2,2,36,256]{3,2,1,0:T(8,128)(2,1)S(1)} collective-permute-done((bf16[2,2,36,256]{3,2,1,0:T(8,128)(2,1)S(1)}, bf16[2,2,36,256]{3,2,1,0:T(8,128)(2,1)S(1)}, u32[]{:S(2)}, u32[]{:S(2)}) %collective-permute-start.3) | collective-permute-done | bytes 73760 | tf_op jit(solution)/shard_map/while/body/eval_jaxpr/ppermute | solution.py:20
  61.9 1.9 collective-permute-start.4
  64.7 1.7 select_dynamic-update-slice_fusion.2
  66.4 6.0 %collective-permute-done.4 = bf16[2,16,32,256]{3,2,1,0:T(8,128)(2,1)S(1)} collective-permute-done((bf16[2,16,32,256]{3,2,1,0:T(8,128)(2,1)S(1)}, bf16[2,16,32,256]{3,2,1,0:T(8,128)(2,1)S(1)}, u32[]{:S(2)}, u32[]{:S(2)}) %collective-permute-start.4) | collective-permute-done | bytes 524320 | tf_op jit(solution)/shard_map/while/body/eval_jaxpr/ppermute | solution.py:28
  73.5 2.3 collective-permute-start
  75.8 1.3 collective-permute-start.1
  77.4 4.2 %collective-permute-done.1 = bf16[2,16,2,256]{3,2,1,0:T(2,128)(2,1)S(1)} collective-permute-done((bf16[2,16,2,256]{3,2,1,0:T(2,128)(2,1)S(1)}, bf16[2,16,2,256]{3,2,1,0:T(2,128)(2,1)S(1)}, u32[]{:S(2)}, u32[]{:S(2)}) %collective-permute-start.1) | collective-permute-done | bytes 32800 | tf_op jit(solution)/shard_map/while/body/eval_jaxpr/ppermute | solution.py:19
  81.7 1.5 collective-permute-start.2
  83.3 1.4 collective-permute-start.3
  85.7 4.0 %collective-permute-done.3 = bf16[2,2,36,256]{3,2,1,0:T(8,128)(2,1)S(1)} collective-permute-done((bf16[2,2,36,256]{3,2,1,0:T(8,128)(2,1)S(1)}, bf16[2,2,36,256]{3,2,1,0:T(8,128)(2,1)S(1)}, u32[]{:S(2)}, u32[]{:S(2)}) %collective-permute-start.3) | collective-permute-done | bytes 73760 | tf_op jit(solution)/shard_map/while/body/eval_jaxpr/ppermute | solution.py:20
  94.8 1.9 collective-permute-start.4
  97.6 1.7 select_dynamic-update-slice_fusion.2
  99.3 6.0 %collective-permute-done.4 = bf16[2,16,32,256]{3,2,1,0:T(8,128)(2,1)S(1)} collective-permute-done((bf16[2,16,32,256]{3,2,1,0:T(8,128)(2,1)S(1)}, bf16[2,16,32,256]{3,2,1,0:T(8,128)(2,1)S(1)}, u32[]{:S(2)}, u32[]{:S(2)}) %collective-permute-start.4) | collective-permute-done | bytes 524320 | tf_op jit(solution)/shard_map/while/body/eval_jaxpr/ppermute | solution.py:28
  106.4 2.0 collective-permute-start
  108.4 1.3 collective-permute-start.1
  109.9 4.2 %collective-permute-done.1 = bf16[2,16,2,256]{3,2,1,0:T(2,128)(2,1)S(1)} collective-permute-done((bf16[2,16,2,256]{3,2,1,0:T(2,128)(2,1)S(1)}, bf16[2,16,2,256]{3,2,1,0:T(2,128)(2,1)S(1)}, u32[]{:S(2)}, u32[]{:S(2)}) %collective-permute-start.1) | collective-permute-done | bytes 32800 | tf_op jit(solution)/shard_map/while/body/eval_jaxpr/ppermute | solution.py:19
  114.2 1.6 collective-permute-start.2
  115.8 1.4 collective-permute-start.3
  118.3 4.0 %collective-permute-done.3 = bf16[2,2,36,256]{3,2,1,0:T(8,128)(2,1)S(1)} collective-permute-done((bf16[2,2,36,256]{3,2,1,0:T(8,128)(2,1)S(1)}, bf16[2,2,36,256]{3,2,1,0:T(8,128)(2,1)S(1)}, u32[]{:S(2)}, u32[]{:S(2)}) %collective-permute-start.3) | collective-permute-done | bytes 73760 | tf_op jit(solution)/shard_map/while/body/eval_jaxpr/ppermute | solution.py:20
  127.4 1.9 collective-permute-start.4
  130.2 1.7 select_dynamic-update-slice_fusion.2
  131.9 6.0 %collective-permute-done.4 = bf16[2,16,32,256]{3,2,1,0:T(8,128)(2,1)S(1)} collective-permute-done((bf16[2,16,32,256]{3,2,1,0:T(8,128)(2,1)S(1)}, bf16[2,16,32,256]{3,2,1,0:T(8,128)(2,1)S(1)}, u32[]{:S(2)}, u32[]{:S(2)}) %collective-permute-start.4) | collective-permute-done | bytes 524320 | tf_op jit(solution)/shard_map/while/body/eval_jaxpr/ppermute | solution.py:28
  139.0 1.9 collective-permute-start
  140.9 1.3 collective-permute-start.1
  142.5 4.2 %collective-permute-done.1 = bf16[2,16,2,256]{3,2,1,0:T(2,128)(2,1)S(1)} collective-permute-done((bf16[2,16,2,256]{3,2,1,0:T(2,128)(2,1)S(1)}, bf16[2,16,2,256]{3,2,1,0:T(2,128)(2,1)S(1)}, u32[]{:S(2)}, u32[]{:S(2)}) %collective-permute-start.1) | collective-permute-done | bytes 32800 | tf_op jit(solution)/shard_map/while/body/eval_jaxpr/ppermute | solution.py:19
  146.8 1.6 collective-permute-start.2
  148.3 1.4 collective-permute-start.3
  150.8 4.0 %collective-permute-done.3 = bf16[2,2,36,256]{3,2,1,0:T(8,128)(2,1)S(1)} collective-permute-done((bf16[2,2,36,256]{3,2,1,0:T(8,128)(2,1)S(1)}, bf16[2,2,36,256]{3,2,1,0:T(8,128)(2,1)S(1)}, u32[]{:S(2)}, u32[]{:S(2)}) %collective-permute-start.3) | collective-permute-done | bytes 73760 | tf_op jit(solution)/shard_map/while/body/eval_jaxpr/ppermute | solution.py:20
  159.9 1.9 collective-permute-start.4
  162.7 1.7 select_dynamic-update-slice_fusion.2
  164.4 6.0 %collective-permute-done.4 = bf16[2,16,32,256]{3,2,1,0:T(8,128)(2,1)S(1)} collective-permute-done((bf16[2,16,32,256]{3,2,1,0:T(8,128)(2,1)S(1)}, bf16[2,16,32,256]{3,2,1,0:T(8,128)(2,1)S(1)}, u32[]{:S(2)}, u32[]{:S(2)}) %collective-permute-start.4) | collective-permute-done | bytes 524320 | tf_op jit(solution)/shard_map/while/body/eval_jaxpr/ppermute | solution.py:28
  171.5 1.9 collective-permute-start
  173.4 1.3 collective-permute-start.1
  175.0 4.2 %collective-permute-done.1 = bf16[2,16,2,256]{3,2,1,0:T(2,128)(2,1)S(1)} collective-permute-done((bf16[2,16,2,256]{3,2,1,0:T(2,128)(2,1)S(1)}, bf16[2,16,2,256]{3,2,1,0:T(2,128)(2,1)S(1)}, u32[]{:S(2)}, u32[]{:S(2)}) %collective-permute-start.1) | collective-permute-done | bytes 32800 | tf_op jit(solution)/shard_map/while/body/eval_jaxpr/ppermute | solution.py:19
  179.3 1.6 collective-permute-start.2
  180.9 1.4 collective-permute-start.3
  183.3 4.0 %collective-permute-done.3 = bf16[2,2,36,256]{3,2,1,0:T(8,128)(2,1)S(1)} collective-permute-done((bf16[2,2,36,256]{3,2,1,0:T(8,128)(2,1)S(1)}, bf16[2,2,36,256]{3,2,1,0:T(8,128)(2,1)S(1)}, u32[]{:S(2)}, u32[]{:S(2)}) %collective-permute-start.3) | collective-permute-done | bytes 73760 | tf_op jit(solution)/shard_map/while/body/eval_jaxpr/ppermute | solution.py:20
  192.4 1.9 collective-permute-start.4
  195.2 1.7 select_dynamic-update-slice_fusion.2
  196.9 6.0 %collective-permute-done.4 = bf16[2,16,32,256]{3,2,1,0:T(8,128)(2,1)S(1)} collective-permute-done((bf16[2,16,32,256]{3,2,1,0:T(8,128)(2,1)S(1)}, bf16[2,16,32,256]{3,2,1,0:T(8,128)(2,1)S(1)}, u32[]{:S(2)}, u32[]{:S(2)}) %collective-permute-start.4) | collective-permute-done | bytes 524320 | tf_op jit(solution)/shard_map/while/body/eval_jaxpr/ppermute | solution.py:28
  204.0 1.9 collective-permute-start
  207.5 4.2 %collective-permute-done.1 = bf16[2,16,2,256]{3,2,1,0:T(2,128)(2,1)S(1)} collective-permute-done((bf16[2,16,2,256]{3,2,1,0:T(2,128)(2,1)S(1)}, bf16[2,16,2,256]{3,2,1,0:T(2,128)(2,1)S(1)}, u32[]{:S(2)}, u32[]{:S(2)}) %collective-permute-start.1) | collective-permute-done | bytes 32800 | tf_op jit(solution)/shard_map/while/body/eval_jaxpr/ppermute | solution.py:19
  211.8 1.6 collective-permute-start.2
  213.4 1.4 collective-permute-start.3
  215.8 4.0 %collective-permute-done.3 = bf16[2,2,36,256]{3,2,1,0:T(8,128)(2,1)S(1)} collective-permute-done((bf16[2,2,36,256]{3,2,1,0:T(8,128)(2,1)S(1)}, bf16[2,2,36,256]{3,2,1,0:T(8,128)(2,1)S(1)}, u32[]{:S(2)}, u32[]{:S(2)}) %collective-permute-start.3) | collective-permute-done | bytes 73760 | tf_op jit(solution)/shard_map/while/body/eval_jaxpr/ppermute | solution.py:20
  224.9 1.9 collective-permute-start.4
  227.7 1.7 select_dynamic-update-slice_fusion.2
  229.5 6.0 %collective-permute-done.4 = bf16[2,16,32,256]{3,2,1,0:T(8,128)(2,1)S(1)} collective-permute-done((bf16[2,16,32,256]{3,2,1,0:T(8,128)(2,1)S(1)}, bf16[2,16,32,256]{3,2,1,0:T(8,128)(2,1)S(1)}, u32[]{:S(2)}, u32[]{:S(2)}) %collective-permute-start.4) | collective-permute-done | bytes 524320 | tf_op jit(solution)/shard_map/while/body/eval_jaxpr/ppermute | solution.py:28
  (232 shorter events, 60.8 us)
Async XLA Ops:
  3.0 1.6 copy-start
  5.8 3.9 %collective-permute-start = (bf16[2,16,2,256]{3,2,1,0:T(2,128)(2,1)S(1)}, bf16[2,16,2,256]{3,2,1,0:T(2,128)(2,1)S(1)}, u32[]{:S(2)}, u32[]{:S(2)}) collective-permute-start(bf16[2,16,2,256]{3,2,1,0:T(2,128)(2,1)S(1)} %get-tuple-element.337), channel_id=1, source_target_pairs={{2,0},{4,2},{6,4},{3,1},{5,3},{7,5},{10,8},{12,10},{14,12},{11,9},... | collective-permute-start | bytes 98312 | tf_op jit(solution)/shard_map/while/body/eval_jaxpr/ppermute | solution.py:20
  8.1 5.8 %collective-permute-start.1 = (bf16[2,16,2,256]{3,2,1,0:T(2,128)(2,1)S(1)}, bf16[2,16,2,256]{3,2,1,0:T(2,128)(2,1)S(1)}, u32[]{:S(2)}, u32[]{:S(2)}) collective-permute-start(bf16[2,16,2,256]{3,2,1,0:T(2,128)(2,1)S(1)} %get-tuple-element.338), channel_id=1, source_target_pairs={{0,2},{2,4},{4,6},{1,3},{3,5},{5,7},{8,10},{10,12},{12,14},{9,11},... | collective-permute-start | bytes 98312 | tf_op jit(solution)/shard_map/while/body/eval_jaxpr/ppermute | solution.py:19
  14.0 5.9 %collective-permute-start.2 = (bf16[2,2,36,256]{3,2,1,0:T(8,128)(2,1)S(1)}, bf16[2,2,36,256]{3,2,1,0:T(8,128)(2,1)S(1)}, u32[]{:S(2)}, u32[]{:S(2)}) collective-permute-start(bf16[2,2,36,256]{3,2,1,0:T(8,128)(2,1)S(1)} %get-tuple-element.339), channel_id=1, source_target_pairs={{0,1},{2,3},{4,5},{6,7},{8,9},{10,11},{12,13},{14,15},{16,17},{18,... | collective-permute-start | bytes 221192 | tf_op jit(solution)/shard_map/while/body/eval_jaxpr/ppermute | solution.py:19
  17.4 2.2 copy-start.1
  17.4 6.5 %collective-permute-start.3 = (bf16[2,2,36,256]{3,2,1,0:T(8,128)(2,1)S(1)}, bf16[2,2,36,256]{3,2,1,0:T(8,128)(2,1)S(1)}, u32[]{:S(2)}, u32[]{:S(2)}) collective-permute-start(bf16[2,2,36,256]{3,2,1,0:T(8,128)(2,1)S(1)} %get-tuple-element.340), channel_id=1, source_target_pairs={{1,0},{3,2},{5,4},{7,6},{9,8},{11,10},{13,12},{15,14},{17,16},{19,... | collective-permute-start | bytes 221192 | tf_op jit(solution)/shard_map/while/body/eval_jaxpr/ppermute | solution.py:20
  28.9 10.5 %collective-permute-start.4 = (bf16[2,16,32,256]{3,2,1,0:T(8,128)(2,1)S(1)}, bf16[2,16,32,256]{3,2,1,0:T(8,128)(2,1)S(1)}, u32[]{:S(2)}, u32[]{:S(2)}) collective-permute-start(bf16[2,16,32,256]{3,2,1,0:T(8,128)(2,1)S(1)} %fusion.170), channel_id=1, source_target_pairs={{0,8},{8,16},{16,24},{1,9},{9,17},{17,25},{2,10},{10,18},{18,26},{... | collective-permute-start | bytes 1572872 | tf_op jit(solution)/shard_map/while/body/eval_jaxpr/ppermute | solution.py:28
  40.5 4.0 %collective-permute-start = (bf16[2,16,2,256]{3,2,1,0:T(2,128)(2,1)S(1)}, bf16[2,16,2,256]{3,2,1,0:T(2,128)(2,1)S(1)}, u32[]{:S(2)}, u32[]{:S(2)}) collective-permute-start(bf16[2,16,2,256]{3,2,1,0:T(2,128)(2,1)S(1)} %get-tuple-element.337), channel_id=1, source_target_pairs={{2,0},{4,2},{6,4},{3,1},{5,3},{7,5},{10,8},{12,10},{14,12},{11,9},... | collective-permute-start | bytes 98312 | tf_op jit(solution)/shard_map/while/body/eval_jaxpr/ppermute | solution.py:20
  43.0 5.8 %collective-permute-start.1 = (bf16[2,16,2,256]{3,2,1,0:T(2,128)(2,1)S(1)}, bf16[2,16,2,256]{3,2,1,0:T(2,128)(2,1)S(1)}, u32[]{:S(2)}, u32[]{:S(2)}) collective-permute-start(bf16[2,16,2,256]{3,2,1,0:T(2,128)(2,1)S(1)} %get-tuple-element.338), channel_id=1, source_target_pairs={{0,2},{2,4},{4,6},{1,3},{3,5},{5,7},{8,10},{10,12},{12,14},{9,11},... | collective-permute-start | bytes 98312 | tf_op jit(solution)/shard_map/while/body/eval_jaxpr/ppermute | solution.py:19
  48.8 4.0 %collective-permute-start.2 = (bf16[2,2,36,256]{3,2,1,0:T(8,128)(2,1)S(1)}, bf16[2,2,36,256]{3,2,1,0:T(8,128)(2,1)S(1)}, u32[]{:S(2)}, u32[]{:S(2)}) collective-permute-start(bf16[2,2,36,256]{3,2,1,0:T(8,128)(2,1)S(1)} %get-tuple-element.339), channel_id=1, source_target_pairs={{0,1},{2,3},{4,5},{6,7},{8,9},{10,11},{12,13},{14,15},{16,17},{18,... | collective-permute-start | bytes 221192 | tf_op jit(solution)/shard_map/while/body/eval_jaxpr/ppermute | solution.py:19
  50.3 2.2 copy-start.1
  50.4 6.5 %collective-permute-start.3 = (bf16[2,2,36,256]{3,2,1,0:T(8,128)(2,1)S(1)}, bf16[2,2,36,256]{3,2,1,0:T(8,128)(2,1)S(1)}, u32[]{:S(2)}, u32[]{:S(2)}) collective-permute-start(bf16[2,2,36,256]{3,2,1,0:T(8,128)(2,1)S(1)} %get-tuple-element.340), channel_id=1, source_target_pairs={{1,0},{3,2},{5,4},{7,6},{9,8},{11,10},{13,12},{15,14},{17,16},{19,... | collective-permute-start | bytes 221192 | tf_op jit(solution)/shard_map/while/body/eval_jaxpr/ppermute | solution.py:20
  61.9 10.5 %collective-permute-start.4 = (bf16[2,16,32,256]{3,2,1,0:T(8,128)(2,1)S(1)}, bf16[2,16,32,256]{3,2,1,0:T(8,128)(2,1)S(1)}, u32[]{:S(2)}, u32[]{:S(2)}) collective-permute-start(bf16[2,16,32,256]{3,2,1,0:T(8,128)(2,1)S(1)} %fusion.170), channel_id=1, source_target_pairs={{0,8},{8,16},{16,24},{1,9},{9,17},{17,25},{2,10},{10,18},{18,26},{... | collective-permute-start | bytes 1572872 | tf_op jit(solution)/shard_map/while/body/eval_jaxpr/ppermute | solution.py:28
  73.5 3.9 %collective-permute-start = (bf16[2,16,2,256]{3,2,1,0:T(2,128)(2,1)S(1)}, bf16[2,16,2,256]{3,2,1,0:T(2,128)(2,1)S(1)}, u32[]{:S(2)}, u32[]{:S(2)}) collective-permute-start(bf16[2,16,2,256]{3,2,1,0:T(2,128)(2,1)S(1)} %get-tuple-element.337), channel_id=1, source_target_pairs={{2,0},{4,2},{6,4},{3,1},{5,3},{7,5},{10,8},{12,10},{14,12},{11,9},... | collective-permute-start | bytes 98312 | tf_op jit(solution)/shard_map/while/body/eval_jaxpr/ppermute | solution.py:20
  75.8 5.8 %collective-permute-start.1 = (bf16[2,16,2,256]{3,2,1,0:T(2,128)(2,1)S(1)}, bf16[2,16,2,256]{3,2,1,0:T(2,128)(2,1)S(1)}, u32[]{:S(2)}, u32[]{:S(2)}) collective-permute-start(bf16[2,16,2,256]{3,2,1,0:T(2,128)(2,1)S(1)} %get-tuple-element.338), channel_id=1, source_target_pairs={{0,2},{2,4},{4,6},{1,3},{3,5},{5,7},{8,10},{10,12},{12,14},{9,11},... | collective-permute-start | bytes 98312 | tf_op jit(solution)/shard_map/while/body/eval_jaxpr/ppermute | solution.py:19
  81.7 4.0 %collective-permute-start.2 = (bf16[2,2,36,256]{3,2,1,0:T(8,128)(2,1)S(1)}, bf16[2,2,36,256]{3,2,1,0:T(8,128)(2,1)S(1)}, u32[]{:S(2)}, u32[]{:S(2)}) collective-permute-start(bf16[2,2,36,256]{3,2,1,0:T(8,128)(2,1)S(1)} %get-tuple-element.339), channel_id=1, source_target_pairs={{0,1},{2,3},{4,5},{6,7},{8,9},{10,11},{12,13},{14,15},{16,17},{18,... | collective-permute-start | bytes 221192 | tf_op jit(solution)/shard_map/while/body/eval_jaxpr/ppermute | solution.py:19
  83.3 2.2 copy-start.1
  83.3 6.5 %collective-permute-start.3 = (bf16[2,2,36,256]{3,2,1,0:T(8,128)(2,1)S(1)}, bf16[2,2,36,256]{3,2,1,0:T(8,128)(2,1)S(1)}, u32[]{:S(2)}, u32[]{:S(2)}) collective-permute-start(bf16[2,2,36,256]{3,2,1,0:T(8,128)(2,1)S(1)} %get-tuple-element.340), channel_id=1, source_target_pairs={{1,0},{3,2},{5,4},{7,6},{9,8},{11,10},{13,12},{15,14},{17,16},{19,... | collective-permute-start | bytes 221192 | tf_op jit(solution)/shard_map/while/body/eval_jaxpr/ppermute | solution.py:20
  94.8 10.5 %collective-permute-start.4 = (bf16[2,16,32,256]{3,2,1,0:T(8,128)(2,1)S(1)}, bf16[2,16,32,256]{3,2,1,0:T(8,128)(2,1)S(1)}, u32[]{:S(2)}, u32[]{:S(2)}) collective-permute-start(bf16[2,16,32,256]{3,2,1,0:T(8,128)(2,1)S(1)} %fusion.170), channel_id=1, source_target_pairs={{0,8},{8,16},{16,24},{1,9},{9,17},{17,25},{2,10},{10,18},{18,26},{... | collective-permute-start | bytes 1572872 | tf_op jit(solution)/shard_map/while/body/eval_jaxpr/ppermute | solution.py:28
  106.4 3.5 %collective-permute-start = (bf16[2,16,2,256]{3,2,1,0:T(2,128)(2,1)S(1)}, bf16[2,16,2,256]{3,2,1,0:T(2,128)(2,1)S(1)}, u32[]{:S(2)}, u32[]{:S(2)}) collective-permute-start(bf16[2,16,2,256]{3,2,1,0:T(2,128)(2,1)S(1)} %get-tuple-element.337), channel_id=1, source_target_pairs={{2,0},{4,2},{6,4},{3,1},{5,3},{7,5},{10,8},{12,10},{14,12},{11,9},... | collective-permute-start | bytes 98312 | tf_op jit(solution)/shard_map/while/body/eval_jaxpr/ppermute | solution.py:20
  108.4 5.8 %collective-permute-start.1 = (bf16[2,16,2,256]{3,2,1,0:T(2,128)(2,1)S(1)}, bf16[2,16,2,256]{3,2,1,0:T(2,128)(2,1)S(1)}, u32[]{:S(2)}, u32[]{:S(2)}) collective-permute-start(bf16[2,16,2,256]{3,2,1,0:T(2,128)(2,1)S(1)} %get-tuple-element.338), channel_id=1, source_target_pairs={{0,2},{2,4},{4,6},{1,3},{3,5},{5,7},{8,10},{10,12},{12,14},{9,11},... | collective-permute-start | bytes 98312 | tf_op jit(solution)/shard_map/while/body/eval_jaxpr/ppermute | solution.py:19
  114.2 4.0 %collective-permute-start.2 = (bf16[2,2,36,256]{3,2,1,0:T(8,128)(2,1)S(1)}, bf16[2,2,36,256]{3,2,1,0:T(8,128)(2,1)S(1)}, u32[]{:S(2)}, u32[]{:S(2)}) collective-permute-start(bf16[2,2,36,256]{3,2,1,0:T(8,128)(2,1)S(1)} %get-tuple-element.339), channel_id=1, source_target_pairs={{0,1},{2,3},{4,5},{6,7},{8,9},{10,11},{12,13},{14,15},{16,17},{18,... | collective-permute-start | bytes 221192 | tf_op jit(solution)/shard_map/while/body/eval_jaxpr/ppermute | solution.py:19
  115.8 2.2 copy-start.1
  115.8 6.5 %collective-permute-start.3 = (bf16[2,2,36,256]{3,2,1,0:T(8,128)(2,1)S(1)}, bf16[2,2,36,256]{3,2,1,0:T(8,128)(2,1)S(1)}, u32[]{:S(2)}, u32[]{:S(2)}) collective-permute-start(bf16[2,2,36,256]{3,2,1,0:T(8,128)(2,1)S(1)} %get-tuple-element.340), channel_id=1, source_target_pairs={{1,0},{3,2},{5,4},{7,6},{9,8},{11,10},{13,12},{15,14},{17,16},{19,... | collective-permute-start | bytes 221192 | tf_op jit(solution)/shard_map/while/body/eval_jaxpr/ppermute | solution.py:20
  127.4 10.5 %collective-permute-start.4 = (bf16[2,16,32,256]{3,2,1,0:T(8,128)(2,1)S(1)}, bf16[2,16,32,256]{3,2,1,0:T(8,128)(2,1)S(1)}, u32[]{:S(2)}, u32[]{:S(2)}) collective-permute-start(bf16[2,16,32,256]{3,2,1,0:T(8,128)(2,1)S(1)} %fusion.170), channel_id=1, source_target_pairs={{0,8},{8,16},{16,24},{1,9},{9,17},{17,25},{2,10},{10,18},{18,26},{... | collective-permute-start | bytes 1572872 | tf_op jit(solution)/shard_map/while/body/eval_jaxpr/ppermute | solution.py:28
  139.0 3.5 %collective-permute-start = (bf16[2,16,2,256]{3,2,1,0:T(2,128)(2,1)S(1)}, bf16[2,16,2,256]{3,2,1,0:T(2,128)(2,1)S(1)}, u32[]{:S(2)}, u32[]{:S(2)}) collective-permute-start(bf16[2,16,2,256]{3,2,1,0:T(2,128)(2,1)S(1)} %get-tuple-element.337), channel_id=1, source_target_pairs={{2,0},{4,2},{6,4},{3,1},{5,3},{7,5},{10,8},{12,10},{14,12},{11,9},... | collective-permute-start | bytes 98312 | tf_op jit(solution)/shard_map/while/body/eval_jaxpr/ppermute | solution.py:20
  140.9 5.8 %collective-permute-start.1 = (bf16[2,16,2,256]{3,2,1,0:T(2,128)(2,1)S(1)}, bf16[2,16,2,256]{3,2,1,0:T(2,128)(2,1)S(1)}, u32[]{:S(2)}, u32[]{:S(2)}) collective-permute-start(bf16[2,16,2,256]{3,2,1,0:T(2,128)(2,1)S(1)} %get-tuple-element.338), channel_id=1, source_target_pairs={{0,2},{2,4},{4,6},{1,3},{3,5},{5,7},{8,10},{10,12},{12,14},{9,11},... | collective-permute-start | bytes 98312 | tf_op jit(solution)/shard_map/while/body/eval_jaxpr/ppermute | solution.py:19
  146.8 4.0 %collective-permute-start.2 = (bf16[2,2,36,256]{3,2,1,0:T(8,128)(2,1)S(1)}, bf16[2,2,36,256]{3,2,1,0:T(8,128)(2,1)S(1)}, u32[]{:S(2)}, u32[]{:S(2)}) collective-permute-start(bf16[2,2,36,256]{3,2,1,0:T(8,128)(2,1)S(1)} %get-tuple-element.339), channel_id=1, source_target_pairs={{0,1},{2,3},{4,5},{6,7},{8,9},{10,11},{12,13},{14,15},{16,17},{18,... | collective-permute-start | bytes 221192 | tf_op jit(solution)/shard_map/while/body/eval_jaxpr/ppermute | solution.py:19
  148.3 2.2 copy-start.1
  148.3 6.5 %collective-permute-start.3 = (bf16[2,2,36,256]{3,2,1,0:T(8,128)(2,1)S(1)}, bf16[2,2,36,256]{3,2,1,0:T(8,128)(2,1)S(1)}, u32[]{:S(2)}, u32[]{:S(2)}) collective-permute-start(bf16[2,2,36,256]{3,2,1,0:T(8,128)(2,1)S(1)} %get-tuple-element.340), channel_id=1, source_target_pairs={{1,0},{3,2},{5,4},{7,6},{9,8},{11,10},{13,12},{15,14},{17,16},{19,... | collective-permute-start | bytes 221192 | tf_op jit(solution)/shard_map/while/body/eval_jaxpr/ppermute | solution.py:20
  159.9 10.5 %collective-permute-start.4 = (bf16[2,16,32,256]{3,2,1,0:T(8,128)(2,1)S(1)}, bf16[2,16,32,256]{3,2,1,0:T(8,128)(2,1)S(1)}, u32[]{:S(2)}, u32[]{:S(2)}) collective-permute-start(bf16[2,16,32,256]{3,2,1,0:T(8,128)(2,1)S(1)} %fusion.170), channel_id=1, source_target_pairs={{0,8},{8,16},{16,24},{1,9},{9,17},{17,25},{2,10},{10,18},{18,26},{... | collective-permute-start | bytes 1572872 | tf_op jit(solution)/shard_map/while/body/eval_jaxpr/ppermute | solution.py:28
  171.5 3.5 %collective-permute-start = (bf16[2,16,2,256]{3,2,1,0:T(2,128)(2,1)S(1)}, bf16[2,16,2,256]{3,2,1,0:T(2,128)(2,1)S(1)}, u32[]{:S(2)}, u32[]{:S(2)}) collective-permute-start(bf16[2,16,2,256]{3,2,1,0:T(2,128)(2,1)S(1)} %get-tuple-element.337), channel_id=1, source_target_pairs={{2,0},{4,2},{6,4},{3,1},{5,3},{7,5},{10,8},{12,10},{14,12},{11,9},... | collective-permute-start | bytes 98312 | tf_op jit(solution)/shard_map/while/body/eval_jaxpr/ppermute | solution.py:20
  173.4 5.8 %collective-permute-start.1 = (bf16[2,16,2,256]{3,2,1,0:T(2,128)(2,1)S(1)}, bf16[2,16,2,256]{3,2,1,0:T(2,128)(2,1)S(1)}, u32[]{:S(2)}, u32[]{:S(2)}) collective-permute-start(bf16[2,16,2,256]{3,2,1,0:T(2,128)(2,1)S(1)} %get-tuple-element.338), channel_id=1, source_target_pairs={{0,2},{2,4},{4,6},{1,3},{3,5},{5,7},{8,10},{10,12},{12,14},{9,11},... | collective-permute-start | bytes 98312 | tf_op jit(solution)/shard_map/while/body/eval_jaxpr/ppermute | solution.py:19
  179.3 4.0 %collective-permute-start.2 = (bf16[2,2,36,256]{3,2,1,0:T(8,128)(2,1)S(1)}, bf16[2,2,36,256]{3,2,1,0:T(8,128)(2,1)S(1)}, u32[]{:S(2)}, u32[]{:S(2)}) collective-permute-start(bf16[2,2,36,256]{3,2,1,0:T(8,128)(2,1)S(1)} %get-tuple-element.339), channel_id=1, source_target_pairs={{0,1},{2,3},{4,5},{6,7},{8,9},{10,11},{12,13},{14,15},{16,17},{18,... | collective-permute-start | bytes 221192 | tf_op jit(solution)/shard_map/while/body/eval_jaxpr/ppermute | solution.py:19
  180.9 2.2 copy-start.1
  180.9 6.5 %collective-permute-start.3 = (bf16[2,2,36,256]{3,2,1,0:T(8,128)(2,1)S(1)}, bf16[2,2,36,256]{3,2,1,0:T(8,128)(2,1)S(1)}, u32[]{:S(2)}, u32[]{:S(2)}) collective-permute-start(bf16[2,2,36,256]{3,2,1,0:T(8,128)(2,1)S(1)} %get-tuple-element.340), channel_id=1, source_target_pairs={{1,0},{3,2},{5,4},{7,6},{9,8},{11,10},{13,12},{15,14},{17,16},{19,... | collective-permute-start | bytes 221192 | tf_op jit(solution)/shard_map/while/body/eval_jaxpr/ppermute | solution.py:20
  192.4 10.5 %collective-permute-start.4 = (bf16[2,16,32,256]{3,2,1,0:T(8,128)(2,1)S(1)}, bf16[2,16,32,256]{3,2,1,0:T(8,128)(2,1)S(1)}, u32[]{:S(2)}, u32[]{:S(2)}) collective-permute-start(bf16[2,16,32,256]{3,2,1,0:T(8,128)(2,1)S(1)} %fusion.170), channel_id=1, source_target_pairs={{0,8},{8,16},{16,24},{1,9},{9,17},{17,25},{2,10},{10,18},{18,26},{... | collective-permute-start | bytes 1572872 | tf_op jit(solution)/shard_map/while/body/eval_jaxpr/ppermute | solution.py:28
  204.0 3.5 %collective-permute-start = (bf16[2,16,2,256]{3,2,1,0:T(2,128)(2,1)S(1)}, bf16[2,16,2,256]{3,2,1,0:T(2,128)(2,1)S(1)}, u32[]{:S(2)}, u32[]{:S(2)}) collective-permute-start(bf16[2,16,2,256]{3,2,1,0:T(2,128)(2,1)S(1)} %get-tuple-element.337), channel_id=1, source_target_pairs={{2,0},{4,2},{6,4},{3,1},{5,3},{7,5},{10,8},{12,10},{14,12},{11,9},... | collective-permute-start | bytes 98312 | tf_op jit(solution)/shard_map/while/body/eval_jaxpr/ppermute | solution.py:20
  205.9 5.8 %collective-permute-start.1 = (bf16[2,16,2,256]{3,2,1,0:T(2,128)(2,1)S(1)}, bf16[2,16,2,256]{3,2,1,0:T(2,128)(2,1)S(1)}, u32[]{:S(2)}, u32[]{:S(2)}) collective-permute-start(bf16[2,16,2,256]{3,2,1,0:T(2,128)(2,1)S(1)} %get-tuple-element.338), channel_id=1, source_target_pairs={{0,2},{2,4},{4,6},{1,3},{3,5},{5,7},{8,10},{10,12},{12,14},{9,11},... | collective-permute-start | bytes 98312 | tf_op jit(solution)/shard_map/while/body/eval_jaxpr/ppermute | solution.py:19
  211.8 4.0 %collective-permute-start.2 = (bf16[2,2,36,256]{3,2,1,0:T(8,128)(2,1)S(1)}, bf16[2,2,36,256]{3,2,1,0:T(8,128)(2,1)S(1)}, u32[]{:S(2)}, u32[]{:S(2)}) collective-permute-start(bf16[2,2,36,256]{3,2,1,0:T(8,128)(2,1)S(1)} %get-tuple-element.339), channel_id=1, source_target_pairs={{0,1},{2,3},{4,5},{6,7},{8,9},{10,11},{12,13},{14,15},{16,17},{18,... | collective-permute-start | bytes 221192 | tf_op jit(solution)/shard_map/while/body/eval_jaxpr/ppermute | solution.py:19
  213.4 2.2 copy-start.1
  213.4 6.5 %collective-permute-start.3 = (bf16[2,2,36,256]{3,2,1,0:T(8,128)(2,1)S(1)}, bf16[2,2,36,256]{3,2,1,0:T(8,128)(2,1)S(1)}, u32[]{:S(2)}, u32[]{:S(2)}) collective-permute-start(bf16[2,2,36,256]{3,2,1,0:T(8,128)(2,1)S(1)} %get-tuple-element.340), channel_id=1, source_target_pairs={{1,0},{3,2},{5,4},{7,6},{9,8},{11,10},{13,12},{15,14},{17,16},{19,... | collective-permute-start | bytes 221192 | tf_op jit(solution)/shard_map/while/body/eval_jaxpr/ppermute | solution.py:20
  224.9 10.5 %collective-permute-start.4 = (bf16[2,16,32,256]{3,2,1,0:T(8,128)(2,1)S(1)}, bf16[2,16,32,256]{3,2,1,0:T(8,128)(2,1)S(1)}, u32[]{:S(2)}, u32[]{:S(2)}) collective-permute-start(bf16[2,16,32,256]{3,2,1,0:T(8,128)(2,1)S(1)} %fusion.170), channel_id=1, source_target_pairs={{0,8},{8,16},{16,24},{1,9},{9,17},{17,25},{2,10},{10,18},{18,26},{... | collective-permute-start | bytes 1572872 | tf_op jit(solution)/shard_map/while/body/eval_jaxpr/ppermute | solution.py:28
  235.4 0.6 copy-start.2
where the time goes:
time: 238 us; the launch traced here: 236 us
  waiting for transfers between devices  101 us (42%)
  starting transfers between devices  60 us (25%)
  matrix products  28.4 us (12%)
  other arithmetic  27 us (11%)
  local copies, waits for them, and re-layouts  16.8 us (7%)
    ppermute x7, waiting for transfers between devices, from_behind(): return lax.ppermute(value, axis, pairs)  41.8 us
    ppermute x14, waiting for transfers between devices, with_halo(): after = lax.ppermute(first, axis, down)  30.1 us
    ppermute x14, waiting for transfers between devices, with_halo(): before = lax.ppermute(last, axis, up)  29.6 us
    ppermute x14, starting transfers between devices, with_halo(): after = lax.ppermute(first, axis, down)  24.8 us
    ppermute x14, starting transfers between devices, with_halo(): before = lax.ppermute(last, axis, up)  21.8 us
    dot_general x63, matrix products, apply_layer(): jnp.dot(shifted[0].reshape(cell_count, channels), filter_weight[vertical_...  14.3 us
    dot_general x63, matrix products, apply_layer(): jnp.dot(shifted[1].reshape(cell_count, channels), alt_kernel[vertical_off...  14.1 us
    ppermute x7, starting transfers between devices, from_behind(): return lax.ppermute(value, axis, pairs)  13.4 us
  transfers between devices with their start and end apart: 35, of which 28 were waited for; matrix products, arithmetic and copies ran while one was open for 11% of the time, Pallas kernels for 0%

commit v1 on v0

v1 whole, which is shorter than its diff:
```python
import functools

import jax
import jax.numpy as jnp
from jax import lax
from jax.experimental import pallas as pl
from jax.experimental.pallas import tpu as pltpu
from jax.sharding import PartitionSpec as P

DILATION_RATE = 2
TAPS = 3
PIECES = 3
residual_scale = 0.8
MESH = pl.DeviceIdType.MESH


def kernel(cfg, f_ref, w_ref, out_ref, loss_ref, fwin, wall, act, stage, lstage,
           hs_sem, hr_sem, xs_sem, xr_sem, ys_sem, yr_sem, bs_sem, br_sem, cs_sem, cr_sem,
           os_sem, or_sem, ls_sem, lr_sem, loc_sem):
    S, M, R, CL, C, n_col, halo, hb, NR, NC = cfg
    me = lax.axis_index("section")
    col = lax.axis_index("col")
    row = lax.axis_index("row")
    micro = lax.rem(me, M)
    group = S // M
    replica = me // M
    sib = me + 1 - 2 * lax.rem(me, 2)
    pairs = S // 2
    my_pair = me // 2
    low = lax.rem(me, 2)
    other_row = 1 - row
    has_left = col > 0
    has_right = col < n_col - 1

    def at(section=None, c=None, r=None):
        return {
            "section": me if section is None else section,
            "col": col if c is None else c,
            "row": row if r is None else r,
        }

    barrier = pltpu.get_barrier_semaphore()

    def hello(dev):
        pl.semaphore_signal(barrier, inc=1, device_id=dev, device_id_type=MESH)

    for d in range(1, S):
        hello(at(section=lax.rem(me + d, S)))
    hello(at(r=other_row))

    @pl.when(has_left)
    def _():
        hello(at(c=col - 1))
        hello(at(c=col - 1, r=other_row))

    @pl.when(has_right)
    def _():
        hello(at(c=col + 1))
        hello(at(c=col + 1, r=other_row))

    K = w_ref.shape[0]
    half = K // 2
    piece = half // PIECES

    own_w = pltpu.make_async_copy(w_ref, wall.at[me], loc_sem.at[0])
    own_w.start()
    own_f = pltpu.make_async_copy(
        f_ref.at[micro],
        fwin.at[pl.ds(row * halo, R), pl.ds(hb, CL)],
        loc_sem.at[1],
    )
    own_f.start()

    for b in range(2):
        for mem in range(2):
            zeros = jnp.zeros((DILATION_RATE * NC, TAPS * C), jnp.bfloat16)
            act[b, mem, 0 : DILATION_RATE * NC, :] = zeros
            act[b, mem, (DILATION_RATE + NR) * NC :, :] = zeros

    greeted = 1 + (S - 1) + 2 * has_left.astype(jnp.int32) + 2 * has_right.astype(jnp.int32)
    pl.semaphore_wait(barrier, greeted)

    def remote(src, dst, s_sem, r_sem, dev):
        return pltpu.make_async_remote_copy(
            src_ref=src, dst_ref=dst, send_sem=s_sem, recv_sem=r_sem,
            device_id=dev, device_id_type=MESH,
        )

    rows_here = pl.ds(row * halo, R)
    rows_out = pl.ds((1 - row) * (R - halo), halo)
    rows_in = pl.ds(row * R, halo)
    mid = pl.ds(hb, CL)
    lcols, rcols = pl.ds(0, hb), pl.ds(hb + CL, hb)
    first, last = pl.ds(0, hb), pl.ds(CL - hb, hb)
    mine = f_ref.at[micro]
    to_left = remote(mine.at[:, first], fwin.at[rows_here, rcols], hs_sem.at[0], hr_sem.at[0], at(c=col - 1))
    to_right = remote(mine.at[:, last], fwin.at[rows_here, lcols], hs_sem.at[1], hr_sem.at[1], at(c=col + 1))
    to_row = remote(mine.at[rows_out], fwin.at[rows_in, mid], hs_sem.at[2], hr_sem.at[2], at(r=other_row))
    to_dl = remote(mine.at[rows_out, first], fwin.at[rows_in, rcols], hs_sem.at[3], hr_sem.at[3], at(c=col - 1, r=other_row))
    to_dr = remote(mine.at[rows_out, last], fwin.at[rows_in, lcols], hs_sem.at[4], hr_sem.at[4], at(c=col + 1, r=other_row))
    to_row.start()

    @pl.when(has_left)
    def _():
        to_left.start()
        to_dl.start()

    @pl.when(has_right)
    def _():
        to_right.start()
        to_dr.start()

    to_sib = remote(w_ref, wall.at[me], bs_sem, br_sem, at(section=sib))
    to_sib.start()

    def twin(k):
        a, b, res, bit = my_pair, k, 0, 1
        while bit < pairs:
            res = res + bit * lax.rem(a // bit + b // bit, 2)
            bit *= 2
        return 2 * res + low

    def part(h, j):
        return pl.ds(pl.multiple_of(h * half + j * piece, 16), piece)

    xcopies = {}
    for k in range(1, pairs):
        for j in range(PIECES):
            cp = remote(w_ref.at[part(row, j)], wall.at[me, part(row, j)],
                        xs_sem.at[k, j], xr_sem.at[k, j], at(section=twin(k)))
            cp.start()
            xcopies[k, j] = cp

    def gather(k):
        t = twin(k)
        tsib = t + 1 - 2 * low
        ycopies, ccopies = [], []
        for j in range(PIECES):
            slot = wall.at[t, part(row, j)]
            remote(slot, slot, xs_sem.at[k, j], xr_sem.at[k, j], at(section=t)).wait_recv()
            cp = remote(slot, slot, ys_sem.at[k, j], yr_sem.at[k, j], at(r=other_row))
            cp.start()
            ycopies.append(cp)
            cp = remote(slot, slot, cs_sem.at[k, 0, j], cr_sem.at[k, 0, j], at(section=sib))
            cp.start()
            ccopies.append(cp)
        for j in range(PIECES):
            slot = wall.at[t, part(other_row, j)]
            remote(slot, slot, ys_sem.at[k, j], yr_sem.at[k, j], at(r=other_row)).wait_recv()
            cp = remote(slot, slot, cs_sem.at[k, 1, j], cr_sem.at[k, 1, j], at(section=sib))
            cp.start()
            ccopies.append(cp)
        for h in range(2):
            for j in range(PIECES):
                slot = wall.at[tsib, part(row if h == 0 else other_row, j)]
                remote(slot, slot, cs_sem.at[k, h, j], cr_sem.at[k, h, j], at(section=sib)).wait_recv()
        for cp in ycopies + ccopies:
            cp.wait_send()

    own_f.wait()
    to_row.wait()

    @pl.when(has_left)
    def _():
        to_left.wait_send()
        to_dl.wait_send()
        to_right.wait_recv()
        to_dr.wait_recv()

    @pl.when(has_right)
    def _():
        to_right.wait_send()
        to_dr.wait_send()
        to_left.wait_recv()
        to_dl.wait_recv()

    cpos = lax.broadcasted_iota(jnp.int32, (1, NC, C), 1) + (col * CL - halo)
    in_map = jnp.logical_and(cpos >= 0, cpos < n_col * CL)

    def put(b, mem, at_row, y, rows):
        m = rows * NC
        sl = pl.ds(pl.multiple_of((at_row + DILATION_RATE) * NC, 16), m)
        left = pltpu.roll(y, DILATION_RATE, 0).astype(jnp.bfloat16)
        right = pltpu.roll(y, m - DILATION_RATE, 0).astype(jnp.bfloat16)
        center = y.astype(jnp.bfloat16)
        for mm in mem:
            act[b, mm, sl, 0:C] = left if mm == 0 else right
            act[b, mm, sl, C : 2 * C] = center
            act[b, mm, sl, 2 * C : 3 * C] = right if mm == 0 else left

    off = hb - halo
    for i in range(0, NR, 4):
        v = fwin[i : i + 4].astype(jnp.float32)[:, off : off + NC, :]
        v = jnp.where(in_map, v, 0.0)
        put(0, (0, 1), i, v.reshape(4 * NC, C), 4)

    own_w.wait()
    to_sib.wait()

    for l in range(S):
        if l % 2 == 0:
            for k in range(1, pairs):
                @pl.when(twin(k) // 2 == l // 2)
                def _(k=k):
                    gather(k)
        n = NR - DILATION_RATE * (l + 1)
        r0 = row * (NR - n)
        chunk = n // 2
        m = chunk * NC
        cur, nxt = l % 2, (l + 1) % 2
        for q in range(2):
            base = r0 + q * chunk
            ys = []
            for mem in range(2):
                lhs = jnp.concatenate(
                    [act[cur, mem, pl.ds(pl.multiple_of((base + DILATION_RATE * ky) * NC, 16), m), :] for ky in range(TAPS)],
                    axis=1,
                )
                acc = jnp.dot(lhs, wall[l], preferred_element_type=jnp.float32)
                res = act[cur, mem, pl.ds(pl.multiple_of((base + DILATION_RATE) * NC, 16), m), C : 2 * C]
                y = residual_scale * (res.astype(jnp.float32) + jnp.maximum(acc, 0.0))
                y = jnp.where(in_map, y.reshape(chunk, NC, C), 0.0)
                y = y.astype(jnp.bfloat16).astype(jnp.float32)
                if l < S - 1:
                    put(nxt, (mem,), base, y.reshape(m, C), chunk)
                ys.append(y[:, halo : halo + CL, :])
            stage[l, q * chunk : (q + 1) * chunk] = ys[0].astype(jnp.bfloat16)
            d = ys[0] - ys[1]
            lstage[l, q * chunk : (q + 1) * chunk, 0:CL] = jnp.sum(d * d, axis=-1)

        src = stage.at[l, pl.ds(row * (n - R), R)]

        @pl.when(jnp.logical_and(replica == l % group, me != l))
        def _(l=l, src=src):
            remote(src, out_ref.at[micro], os_sem.at[l], or_sem.at[micro], at(section=l)).start()
            remote(lstage.at[l], loss_ref.at[micro], ls_sem.at[l], lr_sem.at[micro], at(section=l)).start()

        @pl.when(jnp.logical_and(replica == l % group, me == l))
        def _(l=l, src=src):
            pltpu.make_async_copy(src, out_ref.at[micro], loc_sem.at[2]).start()
            pltpu.make_async_copy(lstage.at[l], loss_ref.at[micro], loc_sem.at[3]).start()

    for k in range(1, pairs):
        for j in range(PIECES):
            xcopies[k, j].wait_send()

    for l in range(S):
        n = NR - DILATION_RATE * (l + 1)
        src = stage.at[l, pl.ds(row * (n - R), R)]

        @pl.when(jnp.logical_and(replica == l % group, me != l))
        def _(l=l, src=src):
            remote(src, out_ref.at[micro], os_sem.at[l], or_sem.at[micro], at(section=l)).wait_send()
            remote(lstage.at[l], loss_ref.at[micro], ls_sem.at[l], lr_sem.at[micro], at(section=l)).wait_send()

        @pl.when(jnp.logical_and(replica == l % group, me == l))
        def _(l=l, src=src):
            pltpu.make_async_copy(src, out_ref.at[micro], loc_sem.at[2]).wait()
            pltpu.make_async_copy(lstage.at[l], loss_ref.at[micro], loc_sem.at[3]).wait()

    for b in range(M):
        sender = b + M * lax.rem(me, group)

        @pl.when(sender != me)
        def _(b=b, sender=sender):
            remote(out_ref.at[b], out_ref.at[b], os_sem.at[0], or_sem.at[b], at(section=sender)).wait_recv()
            remote(loss_ref.at[b], loss_ref.at[b], ls_sem.at[0], lr_sem.at[b], at(section=sender)).wait_recv()


def local(features, conv_weight, tissue):
    S = lax.axis_size("section")
    n_col = lax.axis_size("col")
    M, R, CL, C = features.shape
    halo = DILATION_RATE * S
    hb = -(-halo // 16) * 16
    NR, NC = R + halo, CL + 2 * halo
    taps = conv_weight.shape[1]
    K = taps * taps * C
    pairs = S // 2
    lanes = -(-CL // 128) * 128
    cfg = (S, M, R, CL, C, n_col, halo, hb, NR, NC)
    anyspec = pl.BlockSpec(memory_space=pl.ANY)
    dma = pltpu.SemaphoreType.DMA
    out, sums = pl.pallas_call(
        functools.partial(kernel, cfg),
        out_shape=(
            jax.ShapeDtypeStruct((M, R, CL, C), jnp.bfloat16),
            jax.ShapeDtypeStruct((M, NR, lanes), jnp.float32),
        ),
        in_specs=[anyspec, anyspec],
        out_specs=(anyspec, anyspec),
        scratch_shapes=[
            pltpu.VMEM((NR, CL + 2 * hb, C), jnp.bfloat16),
            pltpu.VMEM((S, K, C), jnp.bfloat16),
            pltpu.VMEM((2, 2, (NR + 2 * DILATION_RATE) * NC, taps * C), jnp.bfloat16),
            pltpu.VMEM((S, NR, CL, C), jnp.bfloat16),
            pltpu.VMEM((S, NR, lanes), jnp.float32),
            dma((5,)), dma((5,)),
            dma((pairs, PIECES)), dma((pairs, PIECES)),
            dma((pairs, PIECES)), dma((pairs, PIECES)),
            dma, dma,
            dma((pairs, 2, PIECES)), dma((pairs, 2, PIECES)),
            dma((S,)), dma((M,)),
            dma((S,)), dma((M,)),
            dma((4,)),
        ],
        compiler_params=pltpu.CompilerParams(
            collective_id=0, has_side_effects=True, vmem_limit_bytes=60 * 1024 * 1024
        ),
    )(features, conv_weight.reshape(K, C))
    layer = lax.axis_index("section")
    start = lax.axis_index("row") * (halo - DILATION_RATE * (layer + 1))
    own = lax.dynamic_slice_in_dim(sums, start, R, axis=1)[:, :, :CL]
    loss = tissue.astype(jnp.float32) * (own * (1.0 / C))
    return out[None], loss[None]


def solution(mesh):
    return jax.shard_map(
        local,
        mesh=mesh,
        in_specs=(
            P(None, "row", "col", None),
            P("section", None, None, None, None),
            P(None, "row", "col"),
        ),
        out_specs=(P("section", None, "row", "col", None), P("section", None, "row", "col")),
        check_vma=False,
    )
```

time: 238 us -> 53 us (0.22)
  the two profiles are of different devices: /device:TPU:26 before, /device:TPU:19 now
where the time goes in v1:
time: 53 us; the launch traced here: 52.8 us
  Pallas kernels  48.4 us (91%)
  local copies, waits for them, and re-layouts  2.27 us (4%)
  other arithmetic  1.44 us (3%)
  between operations  0.66 us (1%)
    pallas_call x1, Pallas kernels, local(): pl.pallas_call(functools.partial(kernel, cfg), out_shape=(jax.ShapeDtypeS...  48.4 us
    unnamed x3, local copies, waits for them, and re-layouts  2.27 us
    broadcast_in_dim x1, other arithmetic, local(): return (out[None], loss[None])  1.44 us

profile of v1, /device:TPU:19, one launch (start us, length us, event | category | flops | bytes accessed | tf_op | source)
XLA Modules:
  0.0 52.8 jit_solution(1428952228175319590)
XLA Ops:
  0.6 0.0 copy-start
  0.6 48.4 %shard_map.50 = (bf16[4,16,32,256]{3,2,1,0:T(8,128)(2,1)}, f32[4,24,128]{2,1,0:T(8,128)}) custom-call(bf16[4,16,32,256]{3,2,1,0:T(8,128)(2,1)} %f_ref.1, bf16[2304,256]{1,0:T(8,128)(2,1)} %bitcast.4), custom_call_target="tpu_custom_call" | custom-call | tf_op jit(solution)/shard_map/pallas_call | solution.py:284
  49.1 0.0 copy-done
  49.1 1.4 %fusion.1 = f32[1,4,16,32]{3,2,1,0:T(8,128)} fusion(f32[4,24,128]{2,1,0:T(8,128)} %get-tuple-element.5, s32[]{:T(128)S(6)} %select_n.3, s32[4,16,32]{2,1,0:T(8,128)S(1)} %copy-done), kind=kLoop, calls=%fused_computation.2 | loop fusion | flops 6144 | bytes 24580 | tf_op jit(solution)/shard_map/broadcast_in_dim | solution.py:315
  50.5 2.3 %copy.6 = bf16[1,4,16,32,256]{4,3,2,1,0:T(8,128)(2,1)} copy(bf16[1,4,16,32,256]{4,3,2,1,0:T(8,128)(2,1)} %bitcast.5) | data formatting | bytes 2097152
Async XLA Ops:
  0.6 48.5 %copy-start = (s32[4,16,32]{2,1,0:T(8,128)S(1)}, s32[4,16,32]{2,1,0:T(8,128)}, u32[]{:S(2)}) copy-start(s32[4,16,32]{2,1,0:T(8,128)} %param.5) | copy-start | bytes 24580

commit v2 on v1

--- a/solution.py
+++ b/solution.py
@@ -9,7 +9,7 @@
 
 DILATION_RATE = 2
 TAPS = 3
-PIECES = 3
+PIECES = 6
 residual_scale = 0.8
 MESH = pl.DeviceIdType.MESH
 
@@ -123,39 +123,60 @@
     def part(h, j):
         return pl.ds(pl.multiple_of(h * half + j * piece, 16), piece)
 
-    xcopies = {}
-    for k in range(1, pairs):
-        for j in range(PIECES):
-            cp = remote(w_ref.at[part(row, j)], wall.at[me, part(row, j)],
-                        xs_sem.at[k, j], xr_sem.at[k, j], at(section=twin(k)))
-            cp.start()
-            xcopies[k, j] = cp
-
-    def gather(k):
-        t = twin(k)
-        tsib = t + 1 - 2 * low
-        ycopies, ccopies = [], []
-        for j in range(PIECES):
-            slot = wall.at[t, part(row, j)]
-            remote(slot, slot, xs_sem.at[k, j], xr_sem.at[k, j], at(section=t)).wait_recv()
-            cp = remote(slot, slot, ys_sem.at[k, j], yr_sem.at[k, j], at(r=other_row))
-            cp.start()
-            ycopies.append(cp)
-            cp = remote(slot, slot, cs_sem.at[k, 0, j], cr_sem.at[k, 0, j], at(section=sib))
-            cp.start()
-            ccopies.append(cp)
-        for j in range(PIECES):
-            slot = wall.at[t, part(other_row, j)]
-            remote(slot, slot, ys_sem.at[k, j], yr_sem.at[k, j], at(r=other_row)).wait_recv()
-            cp = remote(slot, slot, cs_sem.at[k, 1, j], cr_sem.at[k, 1, j], at(section=sib))
-            cp.start()
-            ccopies.append(cp)
-        for h in range(2):
+    def xcopy(k, j):
+        return remote(w_ref.at[part(row, j)], wall.at[me, part(row, j)],
+                      xs_sem.at[k, j], xr_sem.at[k, j], at(section=twin(k)))
+
+    def send_own():
+        for k in range(1, pairs):
             for j in range(PIECES):
-                slot = wall.at[tsib, part(row if h == 0 else other_row, j)]
-                remote(slot, slot, cs_sem.at[k, h, j], cr_sem.at[k, h, j], at(section=sib)).wait_recv()
-        for cp in ycopies + ccopies:
-            cp.wait_send()
+                xcopy(k, j).start()
+
+    pl.when(low == 0)(send_own)
+
+    def ycopy(t, k, j, h):
+        slot = wall.at[t, part(h, j)]
+        return remote(slot, slot, ys_sem.at[k, j], yr_sem.at[k, j], at(r=other_row))
+
+    def ccopy(t, k, j, first):
+        slot = wall.at[t, part(row if first else other_row, j)]
+        n = 0 if first else 1
+        return remote(slot, slot, cs_sem.at[k, n, j], cr_sem.at[k, n, j], at(section=sib))
+
+    def pass_on(l, pieces):
+        for k in range(1, pairs):
+            @pl.when(twin(k) == l)
+            def _(k=k):
+                for j in pieces:
+                    slot = wall.at[l, part(row, j)]
+                    remote(slot, slot, xs_sem.at[k, j], xr_sem.at[k, j], at(section=l)).wait_recv()
+                    ycopy(l, k, j, row).start()
+                    ccopy(l, k, j, True).start()
+
+    def complete(l):
+        @pl.when(me == l)
+        def _():
+            own_w.wait()
+
+        @pl.when(sib == l)
+        def _():
+            to_sib.wait_recv()
+
+        for k in range(1, pairs):
+            @pl.when(twin(k) == l)
+            def _(k=k):
+                for j in range(PIECES):
+                    ycopy(l, k, j, other_row).wait_recv()
+                    ccopy(l, k, j, False).start()
+
+            @pl.when(twin(k) + 1 - 2 * low == l)
+            def _(k=k):
+                for j in range(PIECES):
+                    ccopy(l, k, j, True).wait_recv()
+                if l == 0:
+                    pl.when(low == 1)(send_own)
+                for j in range(PIECES):
+                    ccopy(l, k, j, False).wait_recv()
 
     own_f.wait()
     to_row.wait()
@@ -174,15 +195,22 @@
         to_left.wait_recv()
         to_dl.wait_recv()
 
-    cpos = lax.broadcasted_iota(jnp.int32, (1, NC, C), 1) + (col * CL - halo)
-    in_map = jnp.logical_and(cpos >= 0, cpos < n_col * CL)
+    def in_map_only(v):
+        return jnp.concatenate(
+            [
+                jnp.where(has_left, v[:, :halo], 0.0),
+                v[:, halo : halo + CL],
+                jnp.where(has_right, v[:, halo + CL :], 0.0),
+            ],
+            axis=1,
+        )
 
     def put(b, mem, at_row, y, rows):
         m = rows * NC
         sl = pl.ds(pl.multiple_of((at_row + DILATION_RATE) * NC, 16), m)
-        left = pltpu.roll(y, DILATION_RATE, 0).astype(jnp.bfloat16)
-        right = pltpu.roll(y, m - DILATION_RATE, 0).astype(jnp.bfloat16)
         center = y.astype(jnp.bfloat16)
+        left = pltpu.roll(center, DILATION_RATE, 0)
+        right = pltpu.roll(center, m - DILATION_RATE, 0)
         for mm in mem:
             act[b, mm, sl, 0:C] = left if mm == 0 else right
             act[b, mm, sl, C : 2 * C] = center
@@ -191,18 +219,15 @@
     off = hb - halo
     for i in range(0, NR, 4):
         v = fwin[i : i + 4].astype(jnp.float32)[:, off : off + NC, :]
-        v = jnp.where(in_map, v, 0.0)
+        v = in_map_only(v)
         put(0, (0, 1), i, v.reshape(4 * NC, C), 4)
 
-    own_w.wait()
-    to_sib.wait()
-
+    early, late = range(PIECES // 2), range(PIECES // 2, PIECES)
+    pass_on(0, range(PIECES))
     for l in range(S):
-        if l % 2 == 0:
-            for k in range(1, pairs):
-                @pl.when(twin(k) // 2 == l // 2)
-                def _(k=k):
-                    gather(k)
+        complete(l)
+        if l < S - 1:
+            pass_on(l + 1, early)
         n = NR - DILATION_RATE * (l + 1)
         r0 = row * (NR - n)
         chunk = n // 2
@@ -210,6 +235,8 @@
         cur, nxt = l % 2, (l + 1) % 2
         for q in range(2):
             base = r0 + q * chunk
+            if q == 1 and l < S - 1:
+                pass_on(l + 1, late)
             ys = []
             for mem in range(2):
                 lhs = jnp.concatenate(
@@ -219,14 +246,22 @@
                 acc = jnp.dot(lhs, wall[l], preferred_element_type=jnp.float32)
                 res = act[cur, mem, pl.ds(pl.multiple_of((base + DILATION_RATE) * NC, 16), m), C : 2 * C]
                 y = residual_scale * (res.astype(jnp.float32) + jnp.maximum(acc, 0.0))
-                y = jnp.where(in_map, y.reshape(chunk, NC, C), 0.0)
+                y = in_map_only(y.reshape(chunk, NC, C))
                 y = y.astype(jnp.bfloat16).astype(jnp.float32)
                 if l < S - 1:
                     put(nxt, (mem,), base, y.reshape(m, C), chunk)
                 ys.append(y[:, halo : halo + CL, :])
             stage[l, q * chunk : (q + 1) * chunk] = ys[0].astype(jnp.bfloat16)
             d = ys[0] - ys[1]
-            lstage[l, q * chunk : (q + 1) * chunk, 0:CL] = jnp.sum(d * d, axis=-1)
+            d = (d * d).reshape(chunk * CL, C)
+            sums = lax.dot_general(
+                jnp.ones((8, C), jnp.float32), d, (((1,), (1,)), ((), ())),
+                preferred_element_type=jnp.float32,
+            )
+            lstage[l, :, q * chunk * CL : (q + 1) * chunk * CL] = sums
+
+        if l == 0:
+            pl.when(me == 1)(send_own)
 
         src = stage.at[l, pl.ds(row * (n - R), R)]
 
@@ -242,7 +277,11 @@
 
     for k in range(1, pairs):
         for j in range(PIECES):
-            xcopies[k, j].wait_send()
+            xcopy(k, j).wait_send()
+            ycopy(twin(k), k, j, row).wait_send()
+            ccopy(twin(k), k, j, True).wait_send()
+            ccopy(twin(k), k, j, False).wait_send()
+    to_sib.wait_send()
 
     for l in range(S):
         n = NR - DILATION_RATE * (l + 1)
@@ -277,7 +316,7 @@
     taps = conv_weight.shape[1]
     K = taps * taps * C
     pairs = S // 2
-    lanes = -(-CL // 128) * 128
+    lanes = -(-NR * CL // 128) * 128
     cfg = (S, M, R, CL, C, n_col, halo, hb, NR, NC)
     anyspec = pl.BlockSpec(memory_space=pl.ANY)
     dma = pltpu.SemaphoreType.DMA
@@ -285,7 +324,7 @@
         functools.partial(kernel, cfg),
         out_shape=(
             jax.ShapeDtypeStruct((M, R, CL, C), jnp.bfloat16),
-            jax.ShapeDtypeStruct((M, NR, lanes), jnp.float32),
+            jax.ShapeDtypeStruct((M, 8, lanes), jnp.float32),
         ),
         in_specs=[anyspec, anyspec],
         out_specs=(anyspec, anyspec),
@@ -294,7 +333,7 @@
             pltpu.VMEM((S, K, C), jnp.bfloat16),
             pltpu.VMEM((2, 2, (NR + 2 * DILATION_RATE) * NC, taps * C), jnp.bfloat16),
             pltpu.VMEM((S, NR, CL, C), jnp.bfloat16),
-            pltpu.VMEM((S, NR, lanes), jnp.float32),
+            pltpu.VMEM((S, 8, lanes), jnp.float32),
             dma((5,)), dma((5,)),
             dma((pairs, PIECES)), dma((pairs, PIECES)),
             dma((pairs, PIECES)), dma((pairs, PIECES)),
@@ -310,7 +349,7 @@
     )(features, conv_weight.reshape(K, C))
     layer = lax.axis_index("section")
     start = lax.axis_index("row") * (halo - DILATION_RATE * (layer + 1))
-    own = lax.dynamic_slice_in_dim(sums, start, R, axis=1)[:, :, :CL]
+    own = lax.dynamic_slice_in_dim(sums[:, 0], start * CL, R * CL, axis=1).reshape(M, R, CL)
     loss = tissue.astype(jnp.float32) * (own * (1.0 / C))
     return out[None], loss[None]
 

time: 53 us -> 48 us (0.906)
  Pallas kernels: 48.4 us -> 43.2 us
  local copies, waits for them, and re-layouts: 2.27 us -> 3.25 us
  other arithmetic: 1.44 us -> 0.73 us
    pallas_call x1, Pallas kernels: 48.4 us -> 43.2 us  [local(): pl.pallas_call(functools.partial(kernel, cfg), out_shape=(jax.ShapeDtypeS...]
    slice x0 -> x1, local copies, waits for them, and re-layouts: none -> 0.9 us  [local(): sums[:, 0]]
    broadcast_in_dim x1, other arithmetic: 1.44 us -> 0.63 us  [local(): return (out[None], loss[None])]
where the time goes in v2:
time: 48 us; the launch traced here: 47.8 us
  Pallas kernels  43.2 us (90%)
  local copies, waits for them, and re-layouts  3.25 us (7%)
  other arithmetic  0.73 us (2%)
  between operations  0.66 us (1%)
    pallas_call x1, Pallas kernels, local(): pl.pallas_call(functools.partial(kernel, cfg), out_shape=(jax.ShapeDtypeS...  43.2 us
    unnamed x3, local copies, waits for them, and re-layouts  2.27 us

profile of v2, /device:TPU:19, one launch (start us, length us, event | category | flops | bytes accessed | tf_op | source)
XLA Modules:
  0.0 47.8 jit_solution(13864468269770981827)
XLA Ops:
  0.6 0.0 copy-start
  0.6 43.2 %shard_map.50 = (bf16[4,16,32,256]{3,2,1,0:T(8,128)(2,1)}, f32[4,8,768]{2,1,0:T(8,128)}) custom-call(bf16[4,16,32,256]{3,2,1,0:T(8,128)(2,1)} %f_ref.1, bf16[2304,256]{1,0:T(8,128)(2,1)} %bitcast.4), custom_call_target="tpu_custom_call" | custom-call | tf_op jit(solution)/shard_map/pallas_call | solution.py:323
  43.8 0.9 %slice.3 = f32[4,1,768]{2,1,0:T(1,128)S(1)} slice(f32[4,8,768]{2,1,0:T(8,128)} %get-tuple-element.5), slice={[0:4], [0:1], [0:768]} | slice | bytes 24576 | tf_op jit(solution)/shard_map/slice | solution.py:352
  44.7 0.1 multiply_reduce_fusion
  44.8 0.1 mul.22
  44.9 0.0 copy-done
  44.9 0.6 %multiply_bitcast_fusion = f32[1,4,16,32]{3,2,1,0:T(8,128)} fusion(f32[4,16,32]{2,1,0:T(8,128)S(1)} %mul.22, s32[4,16,32]{2,1,0:T(8,128)S(1)} %copy-done), kind=kLoop, calls=%fused_computation | loop fusion | flops 4096 | bytes 24576 | tf_op jit(solution)/shard_map/broadcast_in_dim | solution.py:354
  45.5 2.3 %copy.6 = bf16[1,4,16,32,256]{4,3,2,1,0:T(8,128)(2,1)} copy(bf16[1,4,16,32,256]{4,3,2,1,0:T(8,128)(2,1)} %bitcast.5) | data formatting | bytes 2097152
Async XLA Ops:
  0.6 44.3 %copy-start = (s32[4,16,32]{2,1,0:T(8,128)S(1)}, s32[4,16,32]{2,1,0:T(8,128)}, u32[]{:S(2)}) copy-start(s32[4,16,32]{2,1,0:T(8,128)} %param.5) | copy-start | bytes 24580
